TPU v7x, 256 devices: a whole 4x4x8 slice. The times are simulated.
256 devices in a mesh: pair: 64 (over y, z, core), virt: 4 (over x).
Axes of the slice: x: 4, y: 4, z: 8, core: 2. Of those that a mesh axis runs over, the one named last changes fastest.
Arguments:
- amplitudes: bfloat16 [2048, 128, 1024], P('pair', 'virt'), may hold values from -6 to 6
- amp_pairs: int32 [2048], P('pair'), may hold values from 0 to 16383, as said below
- pair_map: int32 [16384], replicated, may hold values from -1 to 511, as said below
- integrals: bfloat16 [512, 2, 1024, 1024], P('pair', None, None, 'virt'), may hold values from -0.1875 to 0.1875
- block_cols: int32 [512, 2], P('pair'), may hold values from 0 to 16383, as said below
- occ_energy: float32 [8192], P('pair'), may hold values from -3 to -0.7
- virt_energy: float32 [4096], replicated, may hold values from 0.3 to 2
Outputs:
- update: bfloat16 [2048, 128, 1024], P('pair', None, 'virt')
Inputs may be any that keep to these rules, and one draw needn't show every extreme that they name: `amp_pairs`: within one occupied tile (tiles k * 32 to k * 32 + 31) the pairs differ and each has a row in pair_map. Consecutive occupied tiles form groups that hold the same set of pairs, and a pair belongs to one group only. `pair_map`: exactly 512 entries are not -1: the rows 0 to 511, once each, at the pairs that occur in amp_pairs. Row u lies on pair index u // 8. The pairs of one occupied tile have at most 1 row on any one pair index, and some reach 1. At most 8 occupied tiles hold the pair of any one row, and some row is held by exactly 8. `block_cols`: the 2 entries of a row differ, and each is a pair of the group of occupied tiles that holds the row's own pair.
All inputs are finite; a program needn't handle non-finite values.
Results may differ from a plain program's by a relative error of at most 0.0049.
Values may be sent and summed in bfloat16 or wider, within the bound.
A program may use at most 128 MiB of HBM per device.

v0:
```python
import jax
import jax.numpy as jnp
from jax import lax
from jax.sharding import PartitionSpec as P

VTILE = 32


def local(amplitudes, amp_pairs, pair_map, integrals, block_cols, occ_energy, virt_energy):
    tile_count = amplitudes.shape[0]
    pair_devices = lax.axis_size("pair")
    virt_devices = lax.axis_size("virt")
    capacity = -(-tile_count // pair_devices)
    row_limit = min(8, pair_devices - pair_devices // 4 + 1)
    local_rows = integrals.shape[0]
    block_count = integrals.shape[1]
    full_width = integrals.shape[2]
    part_width = integrals.shape[3]
    occ_rows = occ_energy.shape[0]
    send_slots = pair_devices * capacity
    row_of_tile = pair_map[amp_pairs]
    present = row_of_tile >= 0
    owner_pair = row_of_tile // local_rows
    order_index = jnp.arange(tile_count, dtype=jnp.int32)
    earlier = (
        (owner_pair[:, None] == owner_pair[None, :])
        & (order_index[None, :] < order_index[:, None])
        & present[None, :]
    )
    slot_rank = jnp.sum(earlier.astype(jnp.int32), axis=1)
    destination = jnp.where(present, owner_pair * capacity + slot_rank, send_slots)
    target_rows = (
        jnp.full((send_slots,), -1, jnp.int32)
        .at[destination]
        .set(row_of_tile % local_rows, mode="drop")
    )
    sender_pairs = jnp.broadcast_to(amp_pairs[None, None, :], (pair_devices, capacity, tile_count))
    local_row_ids = jnp.arange(local_rows, dtype=jnp.int32)
    outgoing = lax.all_gather(amplitudes, "virt", axis=1, tiled=True)
    send_tiles = (
        jnp.zeros((send_slots,) + outgoing.shape[1:], jnp.bfloat16)
        .at[destination]
        .set(outgoing, mode="drop")
    )
    packed = (
        send_tiles.reshape((pair_devices, capacity) + outgoing.shape[1:]),
        target_rows.reshape(pair_devices, capacity),
        sender_pairs,
    )
    arrived = lax.all_to_all(packed[0], "pair", split_axis=0, concat_axis=0, tiled=True)
    arrived_rows = lax.all_to_all(packed[1], "pair", split_axis=0, concat_axis=0, tiled=True)
    arrived_pairs = lax.all_to_all(packed[2], "pair", split_axis=0, concat_axis=0, tiled=True)
    sources = arrived.shape[0]
    item_count = arrived.shape[1]
    slot_total = sources * item_count
    tile_height = arrived.shape[2]
    flat_tiles = arrived.reshape(slot_total, tile_height, full_width)
    flat_rows = arrived_rows.reshape(slot_total)
    flat_pairs = arrived_pairs.reshape(slot_total, tile_count)
    slot_index = jnp.arange(slot_total, dtype=jnp.int32)
    limit_index = jnp.arange(row_limit, dtype=jnp.int32)

    def row_step(row_index, products):
        hit_mask = flat_rows == row_index
        hit_rank = jnp.cumsum(hit_mask.astype(jnp.int32)) - 1
        picked = hit_mask[None, :] & (hit_rank[None, :] == limit_index[:, None])
        occupied = jnp.any(picked, axis=1)
        chosen_slot = jnp.sum(picked.astype(jnp.int32) * slot_index[None, :], axis=1)
        gathered = flat_tiles[chosen_slot].reshape(row_limit * tile_height, full_width)
        row_blocks = lax.dynamic_index_in_dim(integrals, row_index, 0, keepdims=False)
        result = jnp.einsum("kd,mdc->kmc", gathered, row_blocks, preferred_element_type=jnp.float32)
        result = result.astype(jnp.bfloat16).reshape(
            row_limit, tile_height, block_count, part_width
        )
        return products.at[jnp.where(occupied, chosen_slot, slot_total)].set(result, mode="drop")

    empty_products = jnp.zeros((slot_total, tile_height, block_count, part_width), jnp.bfloat16)
    products = lax.fori_loop(0, local_rows, row_step, empty_products)
    row_hot = (flat_rows[:, None] == local_row_ids[None, :]).astype(jnp.int32)
    column_pair = jnp.sum(row_hot[:, :, None] * block_cols[None, :, :], axis=1)
    landing = flat_pairs[:, None, :] == column_pair[:, :, None]
    matched = jnp.any(landing, axis=2) & (flat_rows >= 0)[:, None]
    target = jnp.where(
        matched, jnp.sum(landing.astype(jnp.int32) * order_index[None, None, :], axis=2), tile_count
    )
    returned_back = (
        lax.all_to_all(
            products.reshape(sources, item_count, tile_height, block_count, part_width),
            "pair",
            split_axis=0,
            concat_axis=0,
            tiled=True,
        ),
        lax.all_to_all(
            target.reshape(sources, item_count, block_count),
            "pair",
            split_axis=0,
            concat_axis=0,
            tiled=True,
        ),
    )
    back_tiles, back_targets = returned_back
    landing_hot = (back_targets[None] == order_index[:, None, None, None]).astype(jnp.bfloat16)
    ladder = jnp.einsum(
        "apqm,pqimc->aic", landing_hot, back_tiles, preferred_element_type=jnp.float32
    )
    virt_tiles = virt_energy.shape[0] // VTILE
    energy_table = virt_energy.reshape(virt_tiles, VTILE)
    tile_ids = jnp.arange(virt_tiles, dtype=jnp.int32)
    onehot_first = (amp_pairs[:, None] // virt_tiles == tile_ids[None, :]).astype(jnp.float32)
    onehot_second = (amp_pairs[:, None] % virt_tiles == tile_ids[None, :]).astype(jnp.float32)
    energy_first = jnp.dot(onehot_first, energy_table, precision=lax.Precision.HIGHEST)
    energy_second = jnp.dot(onehot_second, energy_table, precision=lax.Precision.HIGHEST)
    per_device = VTILE // virt_devices
    energy_first = lax.dynamic_slice_in_dim(
        energy_first, lax.axis_index("virt") * per_device, per_device, 1
    )
    denominator = (
        energy_first[:, None, :, None]
        + energy_second[:, None, None, :]
        - occ_energy[None, :, None, None]
    )
    denominator = denominator.reshape(tile_count, occ_rows, part_width)
    return (ladder / denominator).astype(jnp.bfloat16)


def solution(mesh):
    in_specs = (
        P("pair", "virt", None),
        P("pair"),
        P(),
        P("pair", None, None, "virt"),
        P("pair", None),
        P("pair"),
        P(),
    )
    out_specs = P("pair", None, "virt")
    return jax.shard_map(local, mesh=mesh, in_specs=in_specs, out_specs=out_specs, check_vma=False)
```

profile of v0, /device:TPU:1, one launch (start us, length us, event | category | flops | bytes accessed | tf_op | source)
XLA Modules:
  0.0 846.5 jit_solution(6966731193070125893)
XLA Ops:
  9.6 22.2 %all_to_all.29 = s32[64,1,1]{2,1,0:T(1,128)S(1)} all-to-all(s32[64,1,1]{2,1,0:T(1,128)S(1)} %copy.52), channel_id=1, replica_groups=mesh['pair'=64,'virt'=4] {'pair'}, dimensions={0} | all-to-all | bytes 512 | tf_op jit(solution)/shard_map/all_to_all | solution.py:51
  33.2 4.7 all-to-all-start
  37.9 60.8 %all-gather.2.cloned.1.call-done = bf16[32,128,1024]{2,1,0:T(8,128)(2,1)} async-done(((bf16[32,32,1024]{2,1,0:T(8,128)(2,1)}), bf16[32,128,1024]{2,1,0:T(8,128)(2,1)}) %all-gather.2.cloned.1.call-update) | async-done | bytes 8388624 | tf_op jit(solution)/shard_map/all_gather | solution.py:39
  98.6 6.0 broadcast_in_dim.78
  104.6 21.4 %scatter_fusion.1 = bf16[64,128,1024]{2,1,0:T(8,128)(2,1)} fusion(bf16[64,128,1024]{2,1,0:T(8,128)(2,1)} %broadcast_in_dim.78, s32[32]{0:T(128)S(1)} %fusion.30, bf16[32,128,1024]{2,1,0:T(8,128)(2,1)} %all-gather.2.cloned.1.call-done), kind=kCustom, calls=%fused_computation.4 | custom fusion | bytes 25165952 | tf_op jit(solution)/shard_map/scatter | solution.py:43
  126.0 11.2 %all-to-all-start.3 = ((bf16[64,1,128,1024]{3,2,1,0:T(8,128)(2,1)}), bf16[64,1,128,1024]{3,2,1,0:T(8,128)(2,1)}, u32[]{:S(2)}, u32[]{:S(2)}) async-start(bf16[64,1,128,1024]{3,2,1,0:T(8,128)(2,1)} %bitcast.89), calls=%async_computation.3 | async-start | bytes 33554432 | tf_op jit(solution)/shard_map/all_to_all | solution.py:50
  139.4 363.4 %all-to-all-done.3 = bf16[64,1,128,1024]{3,2,1,0:T(8,128)(2,1)} async-done(((bf16[64,1,128,1024]{3,2,1,0:T(8,128)(2,1)}), bf16[64,1,128,1024]{3,2,1,0:T(8,128)(2,1)}, u32[]{:S(2)}, u32[]{:S(2)}) %all-to-all-start.3) | async-done | bytes 16777248 | tf_op jit(solution)/shard_map/all_to_all | solution.py:50
  502.7 6.1 all-to-all-start.2
  508.8 4.3 broadcast_in_dim.47
  513.1 98.7 %while.16 = (s32[]{:T(128)}, bf16[64,128,2,256]{3,1,2,0:T(8,128)(2,1)}, s32[64]{0:T(128)S(1)}, bf16[64,128,1024]{2,1,0:T(8,128)(2,1)}, bf16[8,2,1024,256]{3,2,1,0:T(8,128)(2,1)}, /*index=5*/s32[]{:T(128)}, s32[]{:T(128)}) while((s32[]{:T(128)}, bf16[64,128,2,256]{3,1,2,0:T(8,128)(2,1)}, s32[64]{0:T(128)S(1)}, ...), condition=%wide.region_11.12_spmd.clone, body=%wide.region_6.11_spmd.clone.sunk | while | flops 1074274944 | bytes 13639173 | solution.py:78
  513.7 6.5 gather_fusion
  522.7 2.8 scatter_fusion
  526.1 6.5 gather_fusion
  538.4 6.5 gather_fusion
  550.7 6.5 gather_fusion
  559.7 2.8 scatter_fusion
  563.1 6.5 gather_fusion
  575.3 6.5 gather_fusion
  587.7 6.5 gather_fusion
  600.0 6.5 gather_fusion
  611.7 16.3 %copy.67 = bf16[64,128,2,256]{3,2,1,0:T(2,128)(2,1)} copy(bf16[64,128,2,256]{3,1,2,0:T(8,128)(2,1)} %get-tuple-element.181) | data formatting | bytes 16777216 | tf_op jit(solution)/shard_map/while | solution.py:78
  628.0 10.5 %all-to-all-start.4 = ((bf16[64,1,128,2,256]{4,3,2,1,0:T(2,128)(2,1)}), bf16[64,1,128,2,256]{4,3,2,1,0:T(2,128)(2,1)}, u32[]{:S(2)}, u32[]{:S(2)}) async-start(bf16[64,1,128,2,256]{4,3,2,1,0:T(2,128)(2,1)} %bitcast.91), calls=%async_computation.4 | async-start | bytes 16777216 | tf_op jit(solution)/shard_map/all_to_all | solution.py:87
  639.4 184.9 %all-to-all-done.4 = bf16[64,1,128,2,256]{4,3,2,1,0:T(2,128)(2,1)} async-done(((bf16[64,1,128,2,256]{4,3,2,1,0:T(2,128)(2,1)}), bf16[64,1,128,2,256]{4,3,2,1,0:T(2,128)(2,1)}, u32[]{:S(2)}, u32[]{:S(2)}) %all-to-all-start.4) | async-done | bytes 8388640 | tf_op jit(solution)/shard_map/all_to_all | solution.py:87
  824.3 12.9 %fusion.15 = bf16[32,128,256]{2,0,1:T(8,128)(2,1)S(1)} fusion(bf16[64,1,128,2,256]{4,3,2,1,0:T(2,128)(2,1)} %all-to-all-done.4, f32[128]{0:T(128)S(1)} %copy-done.4, f32[32,256]{1,0:T(8,128)S(1)} %add.165, s32[64,2]{0,1:T(2,128)S(1)} %bitcast.94), kind=kOutput, calls=%fused_computation.30 | convolution fusion | flops 271585280 | bytes 10519552 | tf_op jit(solution)/shard_map/apqm,pqimc->aic/dot_general | solution.py:104
  (128 shorter events, 51.0 us)
Async XLA Ops:
  6.5 1.4 copy-start
  6.5 92.1 %all-gather.2.cloned.1.call-start = ((), (), s32[]{:S(2)}) async-start(), calls=%async_computation.5 | async-start | bytes 10485760 | tf_op jit(solution)/shard_map/all_gather | solution.py:39
  33.2 92.8 %all-to-all-start = ((s32[64,1,32]{2,1,0:T(1,128)}), s32[64,1,32]{2,1,0:T(1,128)S(1)}, u32[]{:S(2)}, u32[]{:S(2)}) async-start(s32[64,1,32]{2,1,0:T(1,128)} %broadcast_in_dim.42), calls=%async_computation | async-start | bytes 65536 | tf_op jit(solution)/shard_map/all_to_all | solution.py:52
  126.0 12.4 %copy-start.3 = (s32[8,2]{0,1:T(2,128)S(1)}, s32[8,2]{0,1:T(2,128)}, u32[]{:S(2)}) copy-start(s32[8,2]{0,1:T(2,128)} %param.13) | copy-start | bytes 196
  126.0 376.7 %all-to-all-start.3 = ((bf16[64,1,128,1024]{3,2,1,0:T(8,128)(2,1)}), bf16[64,1,128,1024]{3,2,1,0:T(8,128)(2,1)}, u32[]{:S(2)}, u32[]{:S(2)}) async-start(bf16[64,1,128,1024]{3,2,1,0:T(8,128)(2,1)} %bitcast.89), calls=%async_computation.3 | async-start | bytes 33554432 | tf_op jit(solution)/shard_map/all_to_all | solution.py:50
  502.7 125.3 %all-to-all-start.2 = ((s32[64,1,2]{2,1,0:T(1,128)}), s32[64,1,2]{2,1,0:T(1,128)S(1)}, u32[]{:S(2)}, u32[]{:S(2)}) async-start(s32[64,1,2]{2,1,0:T(1,128)} %copy.53), calls=%async_computation.2 | async-start | bytes 65536 | tf_op jit(solution)/shard_map/all_to_all | solution.py:94
  628.0 10.5 %copy-start.2 = (f32[4096]{0:T(1024)S(1)}, f32[4096]{0:T(1024)}, u32[]{:S(2)}) copy-start(f32[4096]{0:T(1024)} %param.15) | copy-start | bytes 49156
  628.0 196.3 %copy-start.4 = (f32[128]{0:T(128)S(1)}, f32[128]{0:T(128)}, u32[]{:S(2)}) copy-start(f32[128]{0:T(128)} %param.14) | copy-start | bytes 1540
  628.0 196.2 %all-to-all-start.4 = ((bf16[64,1,128,2,256]{4,3,2,1,0:T(2,128)(2,1)}), bf16[64,1,128,2,256]{4,3,2,1,0:T(2,128)(2,1)}, u32[]{:S(2)}, u32[]{:S(2)}) async-start(bf16[64,1,128,2,256]{4,3,2,1,0:T(2,128)(2,1)} %bitcast.91), calls=%async_computation.4 | async-start | bytes 16777216 | tf_op jit(solution)/shard_map/all_to_all | solution.py:87
  824.3 15.4 %copy-start.1 = (s32[16384]{0:T(1024)S(1)}, s32[16384]{0:T(1024)}, u32[]{:S(2)}) copy-start(s32[16384]{0:T(1024)} %param.11) | copy-start | bytes 196612
Sparse Core Ops, SparseCore 0:
  9.2 89.4 all-gather.1
where the time goes:
time: 848 us; the launch traced here: 847 us
  waiting for transfers between devices  610 us (72%)
  local copies, waits for them, and re-layouts  129 us (15%)
  matrix products  33.1 us (4%)
  starting transfers between devices  32.4 us (4%)
  blocking collectives  22.2 us (3%)
  between operations  13.5 us (2%)
    all_to_all x1, waiting for transfers between devices, local(): lax.all_to_all(packed[0], 'pair', split_axis=0, concat_axis=0, tiled=True)  363 us
    all_to_all x1, waiting for transfers between devices, local(): lax.all_to_all(products.reshape(sources, item_count, tile_height, block_c...  185 us
    all_gather x1, waiting for transfers between devices, local(): outgoing = lax.all_gather(amplitudes, 'virt', axis=1, tiled=True)  60.8 us
    gather x8, local copies, waits for them, and re-layouts, row_step(): flat_tiles[chosen_slot].reshape(row_limit * tile_height, full_width)  51.6 us
    all_to_all x1, blocking collectives, local(): lax.all_to_all(packed[1], 'pair', split_axis=0, concat_axis=0, tiled=True)  22.2 us
    scatter x8, local copies, waits for them, and re-layouts, row_step(): products.at[jnp.where(occupied, chosen_slot, slot_total)]  21.9 us
    scatter x1, local copies, waits for them, and re-layouts, local(): send_tiles = jnp.zeros((send_slots,) + outgoing.shape[1:], jnp.bfloat16)....  21.4 us
    dot_general x8, matrix products, row_step(): jnp.einsum('kd,mdc->kmc', gathered, row_blocks, preferred_element_type=jn...  19.8 us
  transfers between devices with their start and end apart: 5, of which 3 were waited for; matrix products, arithmetic and copies ran while one was open for 18% of the time, Pallas kernels for 0%

commit v1 on v0

--- a/solution.py
+++ b/solution.py
@@ -36,7 +36,12 @@
     )
     sender_pairs = jnp.broadcast_to(amp_pairs[None, None, :], (pair_devices, capacity, tile_count))
     local_row_ids = jnp.arange(local_rows, dtype=jnp.int32)
-    outgoing = lax.all_gather(amplitudes, "virt", axis=1, tiled=True)
+    ring = [amplitudes]
+    for hop in range(3):
+        ring.append(lax.ppermute(ring[-1], "virt", [(dev, (dev + 1) % 4) for dev in range(4)]))
+    outgoing = jnp.roll(
+        jnp.concatenate(ring[::-1], axis=1), (lax.axis_index("virt") + 1) * ring[0].shape[1], axis=1
+    )
     send_tiles = (
         jnp.zeros((send_slots,) + outgoing.shape[1:], jnp.bfloat16)
         .at[destination]

time: 848 us -> 928 us (1.094)
  waiting for transfers between devices: 610 us -> 663 us
  starting transfers between devices: 32.4 us -> 66.8 us
  local copies, waits for them, and re-layouts: 129 us -> 157 us
  blocking collectives: 22.2 us -> 0 us
  between operations: 13.5 us -> 0.19 us
    ppermute x0 -> x3, waiting for transfers between devices: none -> 114 us  [local(): lax.ppermute(ring[-1], 'virt', [(dev, (dev + 1) % 4) for dev in range(4)])]
    all_gather x1 -> x0, waiting for transfers between devices: 60.8 us -> none  [local(): outgoing = lax.all_gather(amplitudes, 'virt', axis=1, tiled=True)]
    all_to_all x1 -> x0, blocking collectives: 22.2 us -> none  [local(): lax.all_to_all(packed[1], 'pair', split_axis=0, concat_axis=0, tiled=True)]
    unnamed x10 -> x25, local copies, waits for them, and re-layouts: 0.02 us -> 18.3 us
    all_to_all x0 -> x1, starting transfers between devices: none -> 16 us  [local(): lax.all_to_all(packed[1], 'pair', split_axis=0, concat_axis=0, tiled=True)]
    all_to_all x1, starting transfers between devices: 4.69 us -> 18.9 us  [local(): lax.all_to_all(packed[2], 'pair', split_axis=0, concat_axis=0, tiled=True)]
  transfers between devices with their start and end apart: 5 -> 8, of which waited for: 3 -> 5; matrix products, arithmetic and copies ran while one was open for 18% -> 19% of each run, Pallas kernels for 0% -> 0%
where the time goes in v1:
time: 928 us; the launch traced here: 926 us
  waiting for transfers between devices  663 us (71%)
  local copies, waits for them, and re-layouts  157 us (17%)
  starting transfers between devices  66.8 us (7%)
  matrix products  33.1 us (4%)
    all_to_all x1, waiting for transfers between devices, local(): lax.all_to_all(packed[0], 'pair', split_axis=0, concat_axis=0, tiled=True)  363 us
    all_to_all x1, waiting for transfers between devices, local(): lax.all_to_all(products.reshape(sources, item_count, tile_height, block_c...  185 us
    ppermute x3, waiting for transfers between devices, local(): lax.ppermute(ring[-1], 'virt', [(dev, (dev + 1) % 4) for dev in range(4)])  114 us
    gather x8, local copies, waits for them, and re-layouts, row_step(): flat_tiles[chosen_slot].reshape(row_limit * tile_height, full_width)  51.6 us
    scatter x8, local copies, waits for them, and re-layouts, row_step(): products.at[jnp.where(occupied, chosen_slot, slot_total)]  21.9 us
    scatter x1, local copies, waits for them, and re-layouts, local(): send_tiles = jnp.zeros((send_slots,) + outgoing.shape[1:], jnp.bfloat16)....  21.4 us
    dot_general x8, matrix products, row_step(): jnp.einsum('kd,mdc->kmc', gathered, row_blocks, preferred_element_type=jn...  19.8 us
    all_to_all x1, starting transfers between devices, local(): lax.all_to_all(packed[2], 'pair', split_axis=0, concat_axis=0, tiled=True)  18.9 us
  transfers between devices with their start and end apart: 8, of which 5 were waited for; matrix products, arithmetic and copies ran while one was open for 19% of the time, Pallas kernels for 0%

profile of v1, /device:TPU:1, one launch (start us, length us, event | category | flops | bytes accessed | tf_op | source)
XLA Modules:
  0.0 926.1 jit_solution(9679516669906909615)
XLA Ops:
  2.0 44.6 %collective-permute-done = bf16[32,32,1024]{2,1,0:T(8,128)(2,1)S(1)} collective-permute-done((bf16[32,32,1024]{2,1,0:T(8,128)(2,1)}, bf16[32,32,1024]{2,1,0:T(8,128)(2,1)S(1)}, u32[]{:S(2)}, u32[]{:S(2)}) %collective-permute-start) | collective-permute-done | bytes 2097184 | tf_op jit(solution)/shard_map/ppermute | solution.py:41
  49.8 44.6 %collective-permute-done.1 = bf16[32,32,1024]{2,1,0:T(8,128)(2,1)} collective-permute-done((bf16[32,32,1024]{2,1,0:T(8,128)(2,1)S(1)}, bf16[32,32,1024]{2,1,0:T(8,128)(2,1)}, u32[]{:S(2)}, u32[]{:S(2)}) %collective-permute-start.1) | collective-permute-done | bytes 2097184 | tf_op jit(solution)/shard_map/ppermute | solution.py:41
  98.1 16.0 %all-to-all-start.1 = ((s32[64,1,1]{2,1,0:T(1,128)}), s32[64,1,1]{2,1,0:T(1,128)S(1)}, u32[]{:S(2)}, u32[]{:S(2)}) async-start(s32[64,1,1]{2,1,0:T(1,128)} %copy.52), calls=%async_computation.1 | async-start | bytes 65536 | tf_op jit(solution)/shard_map/all_to_all | solution.py:56
  114.1 25.2 %collective-permute-done.2 = bf16[32,32,1024]{2,1,0:T(8,128)(2,1)} collective-permute-done((bf16[32,32,1024]{2,1,0:T(8,128)(2,1)}, bf16[32,32,1024]{2,1,0:T(8,128)(2,1)}, u32[]{:S(2)}, u32[]{:S(2)}) %collective-permute-start.2) | collective-permute-done | bytes 2097184 | tf_op jit(solution)/shard_map/ppermute | solution.py:41
  158.4 18.9 %all-to-all-start = ((s32[64,1,32]{2,1,0:T(1,128)}), s32[64,1,32]{2,1,0:T(1,128)S(1)}, u32[]{:S(2)}, u32[]{:S(2)}) async-start(s32[64,1,32]{2,1,0:T(1,128)} %broadcast_in_dim.42), calls=%async_computation | async-start | bytes 65536 | tf_op jit(solution)/shard_map/all_to_all | solution.py:57
  177.3 8.2 constant_dynamic-slice_fusion.1
  185.5 6.0 broadcast_in_dim.78
  191.5 21.4 %scatter_fusion.1 = bf16[64,128,1024]{2,1,0:T(8,128)(2,1)} fusion(bf16[64,128,1024]{2,1,0:T(8,128)(2,1)} %broadcast_in_dim.78, s32[32]{0:T(128)S(1)} %fusion.30, bf16[32,128,1024]{2,1,0:T(8,128)(2,1)} %constant_dynamic-slice_fusion.1), kind=kCustom, calls=%fused_computation.4 | custom fusion | bytes 25165952 | tf_op jit(solution)/shard_map/scatter | solution.py:48
  212.9 10.8 %all-to-all-start.3 = ((bf16[64,1,128,1024]{3,2,1,0:T(8,128)(2,1)}), bf16[64,1,128,1024]{3,2,1,0:T(8,128)(2,1)}, u32[]{:S(2)}, u32[]{:S(2)}) async-start(bf16[64,1,128,1024]{3,2,1,0:T(8,128)(2,1)} %bitcast.89), calls=%async_computation.3 | async-start | bytes 33554432 | tf_op jit(solution)/shard_map/all_to_all | solution.py:55
  225.8 363.4 %all-to-all-done.3 = bf16[64,1,128,1024]{3,2,1,0:T(8,128)(2,1)} async-done(((bf16[64,1,128,1024]{3,2,1,0:T(8,128)(2,1)}), bf16[64,1,128,1024]{3,2,1,0:T(8,128)(2,1)}, u32[]{:S(2)}, u32[]{:S(2)}) %all-to-all-start.3) | async-done | bytes 16777248 | tf_op jit(solution)/shard_map/all_to_all | solution.py:55
  589.2 6.1 all-to-all-start.2
  599.6 98.7 %while.16 = (s32[]{:T(128)}, bf16[64,128,2,256]{3,1,2,0:T(8,128)(2,1)}, s32[64]{0:T(128)S(1)}, bf16[64,128,1024]{2,1,0:T(8,128)(2,1)}, bf16[8,2,1024,256]{3,2,1,0:T(8,128)(2,1)}, /*index=5*/s32[]{:T(128)}, s32[]{:T(128)}) while((s32[]{:T(128)}, bf16[64,128,2,256]{3,1,2,0:T(8,128)(2,1)}, s32[64]{0:T(128)S(1)}, ...), condition=%wide.region_11.12_spmd.clone, body=%wide.region_6.11_spmd.clone.sunk | while | flops 1074274944 | bytes 13639173 | solution.py:83
  600.1 6.5 gather_fusion
  612.5 6.5 gather_fusion
  624.8 6.5 gather_fusion
  637.1 6.5 gather_fusion
  649.5 6.5 gather_fusion
  661.8 6.5 gather_fusion
  674.1 6.5 gather_fusion
  686.5 6.5 gather_fusion
  698.2 16.3 %copy.67 = bf16[64,128,2,256]{3,2,1,0:T(2,128)(2,1)} copy(bf16[64,128,2,256]{3,1,2,0:T(8,128)(2,1)} %get-tuple-element.181) | data formatting | bytes 16777216 | tf_op jit(solution)/shard_map/while | solution.py:83
  714.5 10.5 %all-to-all-start.4 = ((bf16[64,1,128,2,256]{4,3,2,1,0:T(2,128)(2,1)}), bf16[64,1,128,2,256]{4,3,2,1,0:T(2,128)(2,1)}, u32[]{:S(2)}, u32[]{:S(2)}) async-start(bf16[64,1,128,2,256]{4,3,2,1,0:T(2,128)(2,1)} %bitcast.91), calls=%async_computation.4 | async-start | bytes 16777216 | tf_op jit(solution)/shard_map/all_to_all | solution.py:92
  725.9 184.9 %all-to-all-done.4 = bf16[64,1,128,2,256]{4,3,2,1,0:T(2,128)(2,1)} async-done(((bf16[64,1,128,2,256]{4,3,2,1,0:T(2,128)(2,1)}), bf16[64,1,128,2,256]{4,3,2,1,0:T(2,128)(2,1)}, u32[]{:S(2)}, u32[]{:S(2)}) %all-to-all-start.4) | async-done | bytes 8388640 | tf_op jit(solution)/shard_map/all_to_all | solution.py:92
  910.7 12.9 %fusion.15 = bf16[32,128,256]{2,0,1:T(8,128)(2,1)S(1)} fusion(bf16[64,1,128,2,256]{4,3,2,1,0:T(2,128)(2,1)} %all-to-all-done.4, f32[128]{0:T(128)S(1)} %copy-done.8, f32[32,256]{1,0:T(8,128)S(1)} %add.181, s32[64,2]{0,1:T(2,128)S(1)} %bitcast.94), kind=kOutput, calls=%fused_computation.30 | convolution fusion | flops 271585280 | bytes 10519552 | tf_op jit(solution)/shard_map/apqm,pqimc->aic/dot_general | solution.py:109
  (149 shorter events, 84.5 us)
Async XLA Ops:
  0.0 95.8 %copy-start = (s32[16384]{0:T(1024)S(1)}, s32[16384]{0:T(1024)}, u32[]{:S(2)}) copy-start(s32[16384]{0:T(1024)} %param.11) | copy-start | bytes 196612
  0.0 147.0 %copy-start.2 = (bf16[32,32,1024]{2,1,0:T(8,128)(2,1)S(1)}, bf16[32,32,1024]{2,1,0:T(8,128)(2,1)}, u32[]{:S(2)}) copy-start(bf16[32,32,1024]{2,1,0:T(8,128)(2,1)} %param.9) | copy-start | bytes 6291460
  0.0 46.6 %collective-permute-start = (bf16[32,32,1024]{2,1,0:T(8,128)(2,1)}, bf16[32,32,1024]{2,1,0:T(8,128)(2,1)S(1)}, u32[]{:S(2)}, u32[]{:S(2)}) collective-permute-start(bf16[32,32,1024]{2,1,0:T(8,128)(2,1)} %param.9), channel_id=1, source_target_pairs={{0,1},{1,2},{2,3},{3,0},{4,5},{5,6},{6,7},{7,4},{8,9},{9,10},{10,1... | collective-permute-start | bytes 6291464 | tf_op jit(solution)/shard_map/ppermute | solution.py:41
  46.6 1.3 copy-start.3
  48.0 46.4 %collective-permute-start.1 = (bf16[32,32,1024]{2,1,0:T(8,128)(2,1)S(1)}, bf16[32,32,1024]{2,1,0:T(8,128)(2,1)}, u32[]{:S(2)}, u32[]{:S(2)}) collective-permute-start(bf16[32,32,1024]{2,1,0:T(8,128)(2,1)S(1)} %collective-permute-done), channel_id=1, source_target_pairs={{0,1},{1,2},{2,3},{3,0},{4,5},{5,6},{6,7},{7,4},{8,9},{9,10},{10,1... | collective-permute-start | bytes 6291464 | tf_op jit(solution)/shard_map/ppermute | solution.py:41
  94.3 45.0 %collective-permute-start.2 = (bf16[32,32,1024]{2,1,0:T(8,128)(2,1)}, bf16[32,32,1024]{2,1,0:T(8,128)(2,1)}, u32[]{:S(2)}, u32[]{:S(2)}) collective-permute-start(bf16[32,32,1024]{2,1,0:T(8,128)(2,1)} %collective-permute-done.1), channel_id=1, source_target_pairs={{0,1},{1,2},{2,3},{3,0},{4,5},{5,6},{6,7},{7,4},{8,9},{9,10},{10,1... | collective-permute-start | bytes 6291464 | tf_op jit(solution)/shard_map/ppermute | solution.py:41
  98.1 59.7 %all-to-all-start.1 = ((s32[64,1,1]{2,1,0:T(1,128)}), s32[64,1,1]{2,1,0:T(1,128)S(1)}, u32[]{:S(2)}, u32[]{:S(2)}) async-start(s32[64,1,1]{2,1,0:T(1,128)} %copy.52), calls=%async_computation.1 | async-start | bytes 65536 | tf_op jit(solution)/shard_map/all_to_all | solution.py:56
  114.1 31.5 %copy-start.4 = (bf16[32,32,1024]{2,1,0:T(8,128)(2,1)S(1)}, bf16[32,32,1024]{2,1,0:T(8,128)(2,1)}, u32[]{:S(2)}) copy-start(bf16[32,32,1024]{2,1,0:T(8,128)(2,1)} %copy-done.3) | copy-start | bytes 6291460
  148.5 9.3 %copy-start.6 = (s32[32]{0:T(128)S(1)}, s32[32]{0:T(128)}, u32[]{:S(2)}) copy-start(s32[32]{0:T(128)} %param.10) | copy-start | bytes 388
  158.4 54.4 %all-to-all-start = ((s32[64,1,32]{2,1,0:T(1,128)}), s32[64,1,32]{2,1,0:T(1,128)S(1)}, u32[]{:S(2)}, u32[]{:S(2)}) async-start(s32[64,1,32]{2,1,0:T(1,128)} %broadcast_in_dim.42), calls=%async_computation | async-start | bytes 65536 | tf_op jit(solution)/shard_map/all_to_all | solution.py:57
  212.9 12.0 %copy-start.7 = (s32[8,2]{0,1:T(2,128)S(1)}, s32[8,2]{0,1:T(2,128)}, u32[]{:S(2)}) copy-start(s32[8,2]{0,1:T(2,128)} %param.13) | copy-start | bytes 196
  212.9 376.3 %all-to-all-start.3 = ((bf16[64,1,128,1024]{3,2,1,0:T(8,128)(2,1)}), bf16[64,1,128,1024]{3,2,1,0:T(8,128)(2,1)}, u32[]{:S(2)}, u32[]{:S(2)}) async-start(bf16[64,1,128,1024]{3,2,1,0:T(8,128)(2,1)} %bitcast.89), calls=%async_computation.3 | async-start | bytes 33554432 | tf_op jit(solution)/shard_map/all_to_all | solution.py:55
  589.2 125.3 %all-to-all-start.2 = ((s32[64,1,2]{2,1,0:T(1,128)}), s32[64,1,2]{2,1,0:T(1,128)S(1)}, u32[]{:S(2)}, u32[]{:S(2)}) async-start(s32[64,1,2]{2,1,0:T(1,128)} %copy.53), calls=%async_computation.2 | async-start | bytes 65536 | tf_op jit(solution)/shard_map/all_to_all | solution.py:99
  714.5 10.5 %copy-start.5 = (f32[4096]{0:T(1024)S(1)}, f32[4096]{0:T(1024)}, u32[]{:S(2)}) copy-start(f32[4096]{0:T(1024)} %param.15) | copy-start | bytes 49156
  714.5 196.2 %copy-start.8 = (f32[128]{0:T(128)S(1)}, f32[128]{0:T(128)}, u32[]{:S(2)}) copy-start(f32[128]{0:T(128)} %param.14) | copy-start | bytes 1540
  714.5 196.2 %all-to-all-start.4 = ((bf16[64,1,128,2,256]{4,3,2,1,0:T(2,128)(2,1)}), bf16[64,1,128,2,256]{4,3,2,1,0:T(2,128)(2,1)}, u32[]{:S(2)}, u32[]{:S(2)}) async-start(bf16[64,1,128,2,256]{4,3,2,1,0:T(2,128)(2,1)} %bitcast.91), calls=%async_computation.4 | async-start | bytes 16777216 | tf_op jit(solution)/shard_map/all_to_all | solution.py:92
  910.7 15.4 %copy-start.1 = (s32[16384]{0:T(1024)S(1)}, s32[16384]{0:T(1024)}, u32[]{:S(2)}) copy-start(s32[16384]{0:T(1024)} %param.11) | copy-start | bytes 196612
